TPU v7x, 256 devices: a whole 4x4x8 slice. The times are simulated.
256 devices in a mesh: seq: 16 (over z, core), mp: 8 (over y, x_hi), dp: 2 (over x_lo).
Axes of the slice: x: 4 (x_hi: 2, x_lo: 2; x = x_hi * 2 + x_lo), y: 4, z: 8, core: 2. Of those that a mesh axis runs over, the one named last changes fastest.
Arguments:
- latents: bfloat16 [2, 3072, 1792], P('dp', 'seq', 'mp'), may hold values from -6 to 6
- grad_out: bfloat16 [2, 3072, 1792], P('dp', 'seq', 'mp'), may hold values from -6 to 6
- sync_mod: bfloat16 [2, 2400, 3584], P('dp', 'seq'), may hold values from -3 to 3
- w_qkv: bfloat16 [1792, 3, 1024], P(None, None, 'mp'), may hold values from -0.125 to 0.125
- w_out: bfloat16 [1024, 1792], P('mp'), may hold values from -0.1875 to 0.1875
- q_gain: float32 [8, 128], P('mp'), may hold values from 0.5 to 2.5
- k_gain: float32 [8, 128], P('mp'), may hold values from 0.5 to 2.5
- frame_of: int32 [2, 3072], P('dp', 'seq'), may hold values from 0 to 2399, as said below
- group_id: int32 [2, 3072], P('dp'), may hold values from 0 to 63, never falling along the last dimension, each value on 1 to 96 neighbouring positions
- clip_len: int32 [2], P('dp'), may hold values from 1536 to 3072
Outputs:
- mixed: bfloat16 [2, 3072, 1792], P('dp', 'seq', 'mp')
- grad_latents: bfloat16 [2, 3072, 1792], P('dp', 'seq', 'mp')
- grad_wqkv: float32 [1792, 3, 1024], P(('seq', 'dp'), None, 'mp')
- grad_wout: float32 [1024, 1792], P('mp', ('seq', 'dp'))
Inputs may be any that keep to these rules, and one draw needn't show every extreme that they name: frame_of[c, l] = floor((96 l + s) / 125) with a phase s of 0 to 124 drawn for each clip, so the latents on seq index j read frames held by seq indices j - 1 and j only.
All inputs are finite; a program needn't handle non-finite values.
Results may differ from a plain program's by a relative error of at most 0.012.
The roundings to bfloat16 on the way count: a program that leaves them out, or rounds other values in their place, can miss the bound.
Values may be sent and summed in bfloat16 or wider, within the bound.
A program may use at most 64 MiB of HBM per device.

v0:
```python
import jax
import jax.numpy as jnp
from jax import lax
from jax.sharding import PartitionSpec as P

EPSILON = 1e-06
NEG_FILL = -1e30


def from_behind(value, axis, steps):
    count = lax.axis_size(axis)
    leading, last = (max(0, -steps), min(count, count - steps))
    return lax.ppermute(value, axis, [(source, source + steps) for source in range(leading, last)])


def inv_rms(values):
    return lax.rsqrt(jnp.mean(values * values, axis=-1, keepdims=True) + EPSILON)


def norm_back(raw, inv_norm, gains, upstream):
    inner_dot = jnp.mean(upstream * gains * raw, axis=-1, keepdims=True)
    return inv_norm * (gains * upstream - raw * inv_norm * inv_norm * inner_dot)


def group_mask(group_ids, clip_length, query_first, query_span, key_span):
    query_group = lax.dynamic_slice_in_dim(group_ids, query_first, query_span, 1)
    key_place = lax.iota(jnp.int32, key_span)
    allowed = (group_ids[:, None, :] <= query_group[:, :, None]) & (
        key_place[None, None, :] < clip_length[:, None, None]
    )
    return allowed[:, None, :, :]


def head_logits(queries, keys, factor):
    return jnp.einsum("cqhd,ckhd->chqk", queries, keys, preferred_element_type=jnp.float32) * factor


def on_device(
    latents, grad_out, sync_mod, w_qkv, w_out, q_gain, k_gain, frame_of, group_id, clip_len
):
    clip_count, row_count, width_part = latents.shape
    frame_count = sync_mod.shape[1]
    model_width = sync_mod.shape[2] // 2
    heads_here, head_dim = q_gain.shape
    inner_width = heads_here * head_dim
    factor = head_dim ** (-0.5)
    seq_place = lax.axis_index("seq")
    model_place = lax.axis_index("mp")
    query_first = seq_place * row_count
    inputs_full, upstream_full = (
        lax.all_gather(latents, "mp", axis=2, tiled=True),
        lax.all_gather(grad_out, "mp", axis=2, tiled=True),
    )
    earlier = from_behind(sync_mod, "seq", 1)
    window = jnp.concatenate([earlier, sync_mod], axis=1)
    local_frame = frame_of - (seq_place * frame_count - frame_count)
    selector = (
        local_frame[:, :, None] == lax.iota(jnp.int32, 2 * frame_count)[None, None, :]
    ).astype(jnp.bfloat16)
    modulation = jnp.einsum("clf,cfe->cle", selector, window, preferred_element_type=jnp.float32)
    mod_scale = modulation[:, :, :model_width]
    mod_gate = modulation[:, :, model_width:]
    inputs_f = inputs_full.astype(jnp.float32)
    inv_norm = inv_rms(inputs_f)
    normed = inputs_f * inv_norm
    hidden = (normed * (1.0 + mod_scale)).astype(jnp.bfloat16)
    flat_hidden = hidden.reshape(clip_count * row_count, model_width)
    flat_weight = w_qkv.reshape(model_width, 3 * inner_width)
    projected = jnp.dot(flat_hidden, flat_weight, preferred_element_type=jnp.float32)
    projected = projected.reshape(clip_count, row_count, 3, heads_here, head_dim)
    query_raw = projected[:, :, 0]
    key_raw = projected[:, :, 1]
    query_inv = inv_rms(query_raw)
    key_inv = inv_rms(key_raw)
    query_norm = (query_raw * query_inv * q_gain).astype(jnp.bfloat16)
    key_norm = (key_raw * key_inv * k_gain).astype(jnp.bfloat16)
    values = projected[:, :, 2].astype(jnp.bfloat16)
    row_max = jnp.full((clip_count, heads_here, row_count), NEG_FILL, jnp.float32)
    key_piece = lax.all_gather(key_norm, "seq", axis=1, tiled=True)
    value_piece = lax.all_gather(values, "seq", axis=1, tiled=True)
    span_len = key_piece.shape[1]
    allowed = group_mask(group_id, clip_len, query_first, row_count, span_len)
    logits = jnp.where(allowed, head_logits(query_norm, key_piece, factor), NEG_FILL)
    new_max = jnp.maximum(row_max, jnp.max(logits, axis=-1))
    unnorm = jnp.where(allowed, jnp.exp(logits - new_max[..., None]), 0.0)
    row_sum = jnp.sum(unnorm, axis=-1)
    row_acc = jnp.einsum(
        "chqk,ckhd->chqd",
        unnorm.astype(jnp.bfloat16),
        value_piece,
        preferred_element_type=jnp.float32,
    )
    row_max, row_sum, row_acc = (new_max, row_sum, row_acc)
    key_all, value_all = (
        lax.all_gather(key_norm, "seq", axis=1, tiled=True),
        lax.all_gather(values, "seq", axis=1, tiled=True),
    )
    heads_out = jnp.transpose(row_acc / row_sum[..., None], (0, 2, 1, 3)).astype(jnp.bfloat16)
    out_rows = heads_out.reshape(clip_count * row_count, inner_width)
    attn_part = jnp.dot(out_rows, w_out, preferred_element_type=jnp.float32).reshape(
        clip_count, row_count, model_width
    )
    attn_mine = lax.psum_scatter(attn_part, "mp", scatter_dimension=2, tiled=True)
    gate_mine = lax.dynamic_slice_in_dim(mod_gate, model_place * width_part, width_part, 2)
    mixed = (latents.astype(jnp.float32) + gate_mine * attn_mine).astype(jnp.bfloat16)
    grad_attn = (upstream_full.astype(jnp.float32) * mod_gate).astype(jnp.bfloat16)
    flat_grad = grad_attn.reshape(clip_count * row_count, model_width)
    grad_wout = jnp.einsum("ti,td->id", out_rows, flat_grad, preferred_element_type=jnp.float32)
    grad_heads = jnp.einsum(
        "td,id->ti", flat_grad, w_out, preferred_element_type=jnp.float32
    ).astype(jnp.bfloat16)
    grad_heads = grad_heads.reshape(clip_count, row_count, heads_here, head_dim)
    out_dot = jnp.transpose(
        jnp.sum(grad_heads.astype(jnp.float32) * heads_out.astype(jnp.float32), axis=-1), (0, 2, 1)
    )
    allowed_all = group_mask(group_id, clip_len, query_first, row_count, key_all.shape[1])
    logits_all = head_logits(query_norm, key_all, factor)
    probs = jnp.where(
        allowed_all, jnp.exp(logits_all - row_max[..., None]) / row_sum[..., None], 0.0
    )
    grad_probs = jnp.einsum(
        "cqhd,ckhd->chqk", grad_heads, value_all, preferred_element_type=jnp.float32
    )
    grad_logits = (probs * (grad_probs - out_dot[..., None])).astype(jnp.bfloat16)
    grad_qnorm = (
        jnp.einsum("chqk,ckhd->cqhd", grad_logits, key_all, preferred_element_type=jnp.float32)
        * factor
    )
    grad_key_all = (
        jnp.einsum("chqk,cqhd->ckhd", grad_logits, query_norm, preferred_element_type=jnp.float32)
        * factor
    )
    grad_value_all = jnp.einsum(
        "chqk,cqhd->ckhd",
        probs.astype(jnp.bfloat16),
        grad_heads,
        preferred_element_type=jnp.float32,
    )
    key_terms = jnp.stack([grad_key_all, grad_value_all], axis=2)
    key_share = lax.psum_scatter(key_terms, "seq", scatter_dimension=1, tiled=True)
    grad_knorm = key_share[:, :, 0]
    grad_values = key_share[:, :, 1]
    grad_query = norm_back(query_raw, query_inv, q_gain, grad_qnorm)
    grad_key = norm_back(key_raw, key_inv, k_gain, grad_knorm)
    grad_proj = jnp.stack([grad_query, grad_key, grad_values], axis=2).astype(jnp.bfloat16)
    grad_proj = grad_proj.reshape(clip_count * row_count, 3 * inner_width)
    grad_wqkv = jnp.einsum(
        "te,tf->ef", flat_hidden, grad_proj, preferred_element_type=jnp.float32
    ).reshape(model_width, 3, inner_width)
    grad_wqkv, grad_wout = (
        lax.psum_scatter(grad_wqkv, ("seq", "dp"), scatter_dimension=0, tiled=True),
        lax.psum_scatter(grad_wout, ("seq", "dp"), scatter_dimension=1, tiled=True),
    )
    grad_hidden = jnp.einsum(
        "tf,ef->te", grad_proj, flat_weight, preferred_element_type=jnp.float32
    )
    grad_hidden = grad_hidden.reshape(clip_count, row_count, model_width)
    grad_full = lax.psum(grad_hidden, "mp")
    grad_normed = grad_full * (1.0 + mod_scale)
    grad_whole = inv_norm * (
        grad_normed - normed * jnp.mean(grad_normed * normed, axis=-1, keepdims=True)
    )
    grad_inputs = lax.dynamic_slice_in_dim(grad_whole, model_place * width_part, width_part, 2)
    grad_latents = (grad_out.astype(jnp.float32) + grad_inputs).astype(jnp.bfloat16)
    return (mixed, grad_latents, grad_wqkv, grad_wout)


def solution(mesh):
    in_specs = (
        P("dp", "seq", "mp"),
        P("dp", "seq", "mp"),
        P("dp", "seq", None),
        P(None, None, "mp"),
        P("mp", None),
        P("mp", None),
        P("mp", None),
        P("dp", "seq"),
        P("dp", None),
        P("dp"),
    )
    out_specs = (
        P("dp", "seq", "mp"),
        P("dp", "seq", "mp"),
        P(("seq", "dp"), None, "mp"),
        P("mp", ("seq", "dp")),
    )
    return jax.shard_map(
        on_device, mesh=mesh, in_specs=in_specs, out_specs=out_specs, check_vma=False
    )
```

profile of v0, /device:TPU:1, one launch (start us, length us, event | category | flops | bytes accessed | tf_op | source)
XLA Modules:
  0.0 658.3 jit_solution(18341032263958154900)
XLA Ops:
  7.2 5.1 collective-permute-start
  15.1 2.6 copy.25
  17.7 41.4 %all_gather.17 = bf16[1,192,1792]{1,0,2:T(2,128)(2,1)S(1)} all-gather(bf16[1,192,224]{1,0,2:T(2,128)(2,1)S(1)} %copy.27), channel_id=1, replica_groups=mesh['seq'=16,'mp'=8,'dp'=2] {'mp'}, dimensions={2}, use_global_device_ids=true | all-gather | bytes 774144 | tf_op jit(solution)/shard_map/all_gather | solution.py:52
  59.0 3.8 copy.28
  62.9 38.2 %all_gather.14 = bf16[1,192,1792]{1,0,2:T(2,128)(2,1)S(1)} all-gather(bf16[1,192,224]{1,0,2:T(2,128)(2,1)S(1)} %copy.23), channel_id=1, replica_groups=mesh['seq'=16,'mp'=8,'dp'=2] {'mp'}, dimensions={2}, use_global_device_ids=true | all-gather | bytes 774144 | tf_op jit(solution)/shard_map/all_gather | solution.py:51
  101.1 4.0 copy.24
  105.9 2.6 convolution_bitcast_fusion
  110.9 28.8 %all-gather = bf16[1,3072,1,1,128]{4,1,2,3,0:T(8,128)(2,1)S(1)} all-gather(bf16[1,192,1,1,128]{4,1,2,3,0:T(8,128)(2,1)S(1)} %slice.67), channel_id=2, replica_groups=mesh['seq'=16,'mp'=8,'dp'=2] {'seq'}, dimensions={1}, use_global_device_ids=true | all-gather | bytes 835584 | tf_op jit(solution)/shard_map/all_gather | solution.py:80
  139.8 17.0 %all_gather.15 = bf16[1,3072,1,128]{3,1,2,0:T(8,128)(2,1)S(1)} all-gather(bf16[1,192,1,128]{3,1,2,0:T(8,128)(2,1)S(1)} %fusion.47), channel_id=1, replica_groups=mesh['seq'=16,'mp'=8,'dp'=2] {'seq'}, dimensions={1}, use_global_device_ids=true | all-gather | bytes 835584 | tf_op jit(solution)/shard_map/all_gather | solution.py:79
  164.2 1.9 pad_maximum_fusion
  166.2 1.4 convolution_bitcast_fusion.3
  167.6 5.1 copy.35
  172.6 2.9 copy.52
  175.8 2.0 fusion.54
  178.7 42.9 %reduce-scatter.10.cloned.1.call-done = f32[1,192,2,1,128]{4,1,2,3,0:T(8,128)} async-done(((f32[1,3072,2,1,128]{4,1,2,3,0:T(8,128)}), f32[1,192,2,1,128]{4,1,2,3,0:T(8,128)}) %reduce-scatter.10.cloned.1.call-update) | async-done | bytes 196624 | tf_op jit(solution)/shard_map/reduce_scatter | solution.py:140
  223.8 3.0 convolution_bitcast_fusion.2
  226.9 2.6 fusion.67
  229.5 3.3 fusion.36
  232.9 72.6 %reduce-scatter.14.cloned.1.call-done = f32[224,192]{1,0:T(8,128)} async-done(((f32[1792,192]{1,0:T(8,128)}), f32[224,192]{1,0:T(8,128)}) %reduce-scatter.14.cloned.1.call-update) | async-done | bytes 172048
  307.4 94.9 %all-reduce.3.cloned.1.call-done = f32[1,192,1792]{2,1,0:T(8,128)} async-done(((f32[1,192,1792]{2,1,0:T(8,128)}), f32[1,192,1792]{2,1,0:T(8,128)}) %all-reduce.3.cloned.1.call-update) | async-done | bytes 1376272 | tf_op jit(solution)/shard_map/psum | solution.py:158
  402.3 2.0 multiply_reduce_fusion
  404.3 1.8 fusion.34
  406.9 119.1 %reduce-scatter.16.cloned.1.call-done = f32[128,56]{0,1:T(8,128)} async-done(((f32[128,1792]{0,1:T(8,128)}), f32[128,56]{0,1:T(8,128)}) %reduce-scatter.16.cloned.1.call-update) | async-done | bytes 28688
  526.1 125.7 %reduce-scatter.12.cloned.1.call-done = f32[56,3,128]{2,0,1:T(8,128)} async-done(((f32[1792,3,128]{2,0,1:T(8,128)}), f32[56,3,128]{2,0,1:T(8,128)}) %reduce-scatter.12.cloned.1.call-update) | async-done | bytes 86032 | tf_op jit(solution)/shard_map/reduce_scatter | solution.py:151
  (92 shorter events, 19.0 us)
Async XLA Ops:
  7.2 150.5 %copy-start = (bf16[128,1792]{1,0:T(8,128)(2,1)S(1)}, bf16[128,1792]{1,0:T(8,128)(2,1)}, u32[]{:S(2)}) copy-start(bf16[128,1792]{1,0:T(8,128)(2,1)} %param.14) | copy-start | bytes 1376260
  7.2 214.4 %reduce-scatter.10.cloned.1.call-start = ((), (), s32[]{:S(2)}) async-start(), calls=%async_computation.4 | async-start | bytes 3342336 | tf_op jit(solution)/shard_map/reduce_scatter | solution.py:140
  7.2 98.2 %collective-permute-start = (bf16[1,150,3584]{2,1,0:T(8,128)(2,1)}, bf16[1,150,3584]{2,1,0:T(8,128)(2,1)}, u32[]{:S(2)}, u32[]{:S(2)}) collective-permute-start(bf16[1,150,3584]{2,1,0:T(8,128)(2,1)} %param.12), channel_id=1, source_target_pairs={{0,16},{16,32},{32,48},{48,64},{64,80},{80,96},{96,112},{112,128},... | collective-permute-start | bytes 3225608 | tf_op jit(solution)/shard_map/ppermute | solution.py:13
  62.9 42.2 %copy-start.15 = (s32[1,3072]{1,0:T(1,128)S(1)}, s32[1,3072]{1,0:T(1,128)}, u32[]{:S(2)}) copy-start(s32[1,3072]{1,0:T(1,128)} %param.18) | copy-start | bytes 36868
  62.9 42.5 %copy-start.20 = (s32[1,192]{1,0:T(1,128)S(1)}, s32[1,192]{1,0:T(1,128)}, u32[]{:S(2)}) copy-start(s32[1,192]{1,0:T(1,128)} %param.17) | copy-start | bytes 2308
  105.4 3.1 copy-start.13
  105.9 2.6 copy-start.3
  109.9 46.9 %copy-start.5 = (bf16[192,1792,1]{1,0,2:T(8,128)(2,1)}, bf16[192,1792,1]{1,0,2:T(8,128)(2,1)S(1)}, u32[]{:S(2)}) copy-start(bf16[192,1792,1]{1,0,2:T(8,128)(2,1)S(1)} %get-tuple-element.8) | copy-start | bytes 2064388
  109.9 29.9 %copy-start.19 = (f32[1,128]{1,0:T(1,128)S(1)}, f32[1,128]{1,0:T(1,128)}, u32[]{:S(2)}) copy-start(f32[1,128]{1,0:T(1,128)} %param.16) | copy-start | bytes 1540
  110.0 46.8 %copy-start.21 = (f32[1,128]{1,0:T(1,128)S(1)}, f32[1,128]{1,0:T(1,128)}, u32[]{:S(2)}) copy-start(f32[1,128]{1,0:T(1,128)} %param.15) | copy-start | bytes 1540
  110.8 46.9 %copy-start.17 = (f32[192]{0:T(256)}, f32[192]{0:T(256)S(1)}, u32[]{:S(2)}) copy-start(f32[192]{0:T(256)S(1)} %add_rsqrt_fusion) | copy-start | bytes 2308
  110.9 51.4 %copy-start.18 = (f32[192]{0:T(256)}, f32[192]{0:T(256)S(1)}, u32[]{:S(2)}) copy-start(f32[192]{0:T(256)S(1)} %add_rsqrt_fusion.1) | copy-start | bytes 2308
  139.8 17.9 %copy-start.4 = (bf16[1,192,1792]{2,1,0:T(8,128)(2,1)S(1)}, bf16[1,192,1792]{2,1,0:T(8,128)(2,1)}, u32[]{:S(2)}) copy-start(bf16[1,192,1792]{2,1,0:T(8,128)(2,1)} %copy.28) | copy-start | bytes 2064388
  161.3 4.9 copy-start.11
  166.1 139.4 %reduce-scatter.14.cloned.1.call-start = ((), (), s32[]{:S(2)}) async-start(), calls=%async_computation.7 | async-start | bytes 2064384
  172.6 3.1 copy-start.22
  175.5 226.8 %all-reduce.3.cloned.1.call-start = ((), (), s32[]{:S(2)}) async-start(), calls=%async_computation.5 | async-start | bytes 2752512 | tf_op jit(solution)/shard_map/psum | solution.py:158
  223.8 3.1 copy-start.12
  226.8 299.2 %reduce-scatter.16.cloned.1.call-start = ((), (), s32[]{:S(2)}) async-start(), calls=%async_computation.8 | async-start | bytes 946176
  229.5 422.3 %reduce-scatter.12.cloned.1.call-start = ((), (), s32[]{:S(2)}) async-start(), calls=%async_computation.6 | async-start | bytes 2838528 | tf_op jit(solution)/shard_map/reduce_scatter | solution.py:151
  232.9 169.4 %copy-start.14 = (f32[192]{0:T(256)S(1)}, f32[192]{0:T(256)}, u32[]{:S(2)}) copy-start(f32[192]{0:T(256)} %copy-done.13) | copy-start | bytes 2308
  307.4 96.9 %copy-start.9 = (bf16[1,192,224]{2,1,0:T(8,128)(2,1)S(1)}, bf16[1,192,224]{2,1,0:T(8,128)(2,1)}, u32[]{:S(2)}) copy-start(bf16[1,192,224]{2,1,0:T(8,128)(2,1)} %param.11) | copy-start | bytes 258052
  307.4 98.8 %copy-start.8 = (f32[1,192,224]{2,1,0:T(8,128)S(1)}, f32[1,192,224]{2,1,0:T(8,128)}, u32[]{:S(2)}) copy-start(f32[1,192,224]{2,1,0:T(8,128)} %copy.36) | copy-start | bytes 516100
  402.3 3.8 copy-start.10
  (5 other events, 5.9 us)
Sparse Core Ops, SparseCore 0:
  166.2 55.2 reduce-scatter.9
  225.6 79.8 reduce-scatter.13
  308.1 94.1 all-reduce.2
  405.2 120.7 reduce-scatter.15
  529.0 122.6 reduce-scatter.11
where the time goes:
time: 659 us; the launch traced here: 658 us
  waiting for transfers between devices  455 us (69%)
  blocking collectives  125 us (19%)
  local copies, waits for them, and re-layouts  24.3 us (4%)
  matrix products  20.9 us (3%)
  between operations  14.8 us (2%)
  other arithmetic  12.2 us (2%)
    unnamed x7, waiting for transfers between devices  192 us
    reduce_scatter x1, waiting for transfers between devices, on_device(): lax.psum_scatter(grad_wqkv, ('seq', 'dp'), scatter_dimension=0, tiled=True)  126 us
    psum x1, waiting for transfers between devices, on_device(): grad_full = lax.psum(grad_hidden, 'mp')  94.9 us
    reduce_scatter x1, waiting for transfers between devices, on_device(): lax.psum_scatter(key_terms, 'seq', scatter_dimension=1, tiled=True)  42.9 us
    all_gather x1, blocking collectives, on_device(): lax.all_gather(grad_out, 'mp', axis=2, tiled=True)  41.4 us
    all_gather x1, blocking collectives, on_device(): lax.all_gather(latents, 'mp', axis=2, tiled=True)  38.2 us
    all_gather x1, blocking collectives, on_device(): value_piece = lax.all_gather(values, 'seq', axis=1, tiled=True)  28.8 us
    all_gather x1, blocking collectives, on_device(): key_piece = lax.all_gather(key_norm, 'seq', axis=1, tiled=True)  17 us
  transfers between devices with their start and end apart: 6, of which 5 were waited for; matrix products, arithmetic and copies ran while one was open for 6% of the time, Pallas kernels for 0%

commit v1 on v0

--- a/solution.py
+++ b/solution.py
@@ -155,7 +155,7 @@
         "tf,ef->te", grad_proj, flat_weight, preferred_element_type=jnp.float32
     )
     grad_hidden = grad_hidden.reshape(clip_count, row_count, model_width)
-    grad_full = lax.psum(grad_hidden, "mp")
+    grad_full = jnp.sum(lax.all_gather(grad_hidden, "mp"), axis=0)
     grad_normed = grad_full * (1.0 + mod_scale)
     grad_whole = inv_norm * (
         grad_normed - normed * jnp.mean(grad_normed * normed, axis=-1, keepdims=True)

time: 659 us -> 694 us (1.053)
  waiting for transfers between devices: 455 us -> 485 us
    all_gather x0 -> x1, waiting for transfers between devices: none -> 135 us  [on_device(): grad_full = jnp.sum(lax.all_gather(grad_hidden, 'mp'), axis=0)]
    psum x1 -> x0, waiting for transfers between devices: 94.9 us -> none  [on_device(): grad_full = lax.psum(grad_hidden, 'mp')]
    all_gather x1, blocking collectives: 17 us -> 28.8 us  [on_device(): key_piece = lax.all_gather(key_norm, 'seq', axis=1, tiled=True)]
    all_gather x1, blocking collectives: 28.8 us -> 17 us  [on_device(): value_piece = lax.all_gather(values, 'seq', axis=1, tiled=True)]
    unnamed x7, waiting for transfers between devices: 192 us -> 181 us
    unnamed x53 -> x55, local copies, waits for them, and re-layouts: 16.3 us -> 15.2 us
  transfers between devices with their start and end apart: 6 -> 6, of which waited for: 5 -> 5; matrix products, arithmetic and copies ran while one was open for 6% -> 7% of each run, Pallas kernels for 0% -> 0%
where the time goes in v1:
time: 694 us; the launch traced here: 693 us
  waiting for transfers between devices  485 us (70%)
  blocking collectives  125 us (18%)
  local copies, waits for them, and re-layouts  23.2 us (3%)
  matrix products  20.9 us (3%)
  other arithmetic  18.5 us (3%)
  between operations  14.9 us (2%)
    unnamed x7, waiting for transfers between devices  181 us
    all_gather x1, waiting for transfers between devices, on_device(): grad_full = jnp.sum(lax.all_gather(grad_hidden, 'mp'), axis=0)  135 us
    reduce_scatter x1, waiting for transfers between devices, on_device(): lax.psum_scatter(grad_wqkv, ('seq', 'dp'), scatter_dimension=0, tiled=True)  126 us
    reduce_scatter x1, waiting for transfers between devices, on_device(): lax.psum_scatter(key_terms, 'seq', scatter_dimension=1, tiled=True)  42.9 us
    all_gather x1, blocking collectives, on_device(): lax.all_gather(latents, 'mp', axis=2, tiled=True)  41.4 us
    all_gather x1, blocking collectives, on_device(): lax.all_gather(grad_out, 'mp', axis=2, tiled=True)  38 us
    all_gather x1, blocking collectives, on_device(): key_piece = lax.all_gather(key_norm, 'seq', axis=1, tiled=True)  28.8 us
    all_gather x1, blocking collectives, on_device(): value_piece = lax.all_gather(values, 'seq', axis=1, tiled=True)  17 us
  transfers between devices with their start and end apart: 6, of which 5 were waited for; matrix products, arithmetic and copies ran while one was open for 7% of the time, Pallas kernels for 0%

profile of v1, /device:TPU:1, one launch (start us, length us, event | category | flops | bytes accessed | tf_op | source)
XLA Modules:
  0.0 693.1 jit_solution(4557736066117866007)
XLA Ops:
  7.2 5.1 collective-permute-start
  13.4 41.4 %all_gather.17 = bf16[1,192,1792]{1,0,2:T(2,128)(2,1)S(1)} all-gather(bf16[1,192,224]{1,0,2:T(2,128)(2,1)S(1)} %copy.23), channel_id=1, replica_groups=mesh['seq'=16,'mp'=8,'dp'=2] {'mp'}, dimensions={2}, use_global_device_ids=true | all-gather | bytes 774144 | tf_op jit(solution)/shard_map/all_gather | solution.py:51
  54.8 4.0 copy.24
  58.7 2.8 copy.25
  62.4 38.0 %all_gather.20 = bf16[1,192,1792]{1,0,2:T(2,128)(2,1)S(1)} all-gather(bf16[1,192,224]{1,0,2:T(2,128)(2,1)S(1)} %copy.27), channel_id=1, replica_groups=mesh['seq'=16,'mp'=8,'dp'=2] {'mp'}, dimensions={2}, use_global_device_ids=true | all-gather | bytes 774144 | tf_op jit(solution)/shard_map/all_gather | solution.py:52
  100.4 3.8 copy.28
  104.6 2.6 convolution_bitcast_fusion
  109.6 28.8 %all_gather.18 = bf16[1,3072,1,128]{3,1,2,0:T(8,128)(2,1)S(1)} all-gather(bf16[1,192,1,128]{3,1,2,0:T(8,128)(2,1)S(1)} %fusion.47), channel_id=1, replica_groups=mesh['seq'=16,'mp'=8,'dp'=2] {'seq'}, dimensions={1}, use_global_device_ids=true | all-gather | bytes 835584 | tf_op jit(solution)/shard_map/all_gather | solution.py:79
  139.5 17.0 %all-gather = bf16[1,3072,1,1,128]{4,1,2,3,0:T(8,128)(2,1)S(1)} all-gather(bf16[1,192,1,1,128]{4,1,2,3,0:T(8,128)(2,1)S(1)} %slice.67), channel_id=2, replica_groups=mesh['seq'=16,'mp'=8,'dp'=2] {'seq'}, dimensions={1}, use_global_device_ids=true | all-gather | bytes 835584 | tf_op jit(solution)/shard_map/all_gather | solution.py:80
  163.1 2.0 pad_maximum_fusion
  166.7 5.1 copy.35
  171.7 2.8 copy.52
  174.8 2.0 fusion.54
  177.7 42.9 %reduce-scatter.10.cloned.1.call-done = f32[1,192,2,1,128]{4,1,2,3,0:T(8,128)} async-done(((f32[1,3072,2,1,128]{4,1,2,3,0:T(8,128)}), f32[1,192,2,1,128]{4,1,2,3,0:T(8,128)}) %reduce-scatter.10.cloned.1.call-update) | async-done | bytes 196624 | tf_op jit(solution)/shard_map/reduce_scatter | solution.py:140
  222.9 3.0 fusion.34
  225.9 2.5 fusion.67
  228.5 3.4 fusion.36
  232.0 72.6 %reduce-scatter.14.cloned.1.call-done = f32[224,192]{1,0:T(8,128)} async-done(((f32[1792,192]{1,0:T(8,128)}), f32[224,192]{1,0:T(8,128)}) %reduce-scatter.14.cloned.1.call-update) | async-done | bytes 172048
  306.5 135.4 %all-gather.4.cloned.1.call-done = f32[1536,1792]{1,0:T(8,128)} async-done(((f32[192,1792]{1,0:T(8,128)}), f32[1536,1792]{1,0:T(8,128)}) %all-gather.4.cloned.1.call-update) | async-done | bytes 11010064 | tf_op jit(solution)/shard_map/all_gather | solution.py:158
  441.9 6.0 reduce.13
  447.9 2.0 multiply_reduce_fusion
  449.9 1.8 fusion.33
  452.5 108.4 %reduce-scatter.16.cloned.1.call-done = f32[128,56]{0,1:T(8,128)} async-done(((f32[128,1792]{0,1:T(8,128)}), f32[128,56]{0,1:T(8,128)}) %reduce-scatter.16.cloned.1.call-update) | async-done | bytes 28688
  560.9 125.7 %reduce-scatter.12.cloned.1.call-done = f32[56,3,128]{2,0,1:T(8,128)} async-done(((f32[1792,3,128]{2,0,1:T(8,128)}), f32[56,3,128]{2,0,1:T(8,128)}) %reduce-scatter.12.cloned.1.call-update) | async-done | bytes 86032 | tf_op jit(solution)/shard_map/reduce_scatter | solution.py:151
  (95 shorter events, 19.1 us)
Async XLA Ops:
  7.2 150.2 %copy-start = (bf16[128,1792]{1,0:T(8,128)(2,1)S(1)}, bf16[128,1792]{1,0:T(8,128)(2,1)}, u32[]{:S(2)}) copy-start(bf16[128,1792]{1,0:T(8,128)(2,1)} %param.14) | copy-start | bytes 1376260
  7.2 213.4 %reduce-scatter.10.cloned.1.call-start = ((), (), s32[]{:S(2)}) async-start(), calls=%async_computation.4 | async-start | bytes 3342336 | tf_op jit(solution)/shard_map/reduce_scatter | solution.py:140
  7.2 97.3 %collective-permute-start = (bf16[1,150,3584]{2,1,0:T(8,128)(2,1)}, bf16[1,150,3584]{2,1,0:T(8,128)(2,1)}, u32[]{:S(2)}, u32[]{:S(2)}) collective-permute-start(bf16[1,150,3584]{2,1,0:T(8,128)(2,1)} %param.12), channel_id=1, source_target_pairs={{0,16},{16,32},{32,48},{48,64},{64,80},{80,96},{96,112},{112,128},... | collective-permute-start | bytes 3225608 | tf_op jit(solution)/shard_map/ppermute | solution.py:13
  54.8 7.5 %copy-start.9 = (bf16[1,192,224]{2,1,0:T(8,128)(2,1)S(1)}, bf16[1,192,224]{2,1,0:T(8,128)(2,1)}, u32[]{:S(2)}) copy-start(bf16[1,192,224]{2,1,0:T(8,128)(2,1)} %param.11) | copy-start | bytes 258052
  58.7 45.6 %copy-start.2 = (bf16[1,192,1792]{2,1,0:T(8,128)(2,1)}, bf16[1,192,1792]{2,1,0:T(8,128)(2,1)S(1)}, u32[]{:S(2)}) copy-start(bf16[1,192,1792]{2,1,0:T(8,128)(2,1)S(1)} %copy.24) | copy-start | bytes 2064388
  62.4 41.8 %copy-start.16 = (s32[1,3072]{1,0:T(1,128)S(1)}, s32[1,3072]{1,0:T(1,128)}, u32[]{:S(2)}) copy-start(s32[1,3072]{1,0:T(1,128)} %param.18) | copy-start | bytes 36868
  62.4 42.1 %copy-start.21 = (s32[1,192]{1,0:T(1,128)S(1)}, s32[1,192]{1,0:T(1,128)}, u32[]{:S(2)}) copy-start(s32[1,192]{1,0:T(1,128)} %param.17) | copy-start | bytes 2308
  104.5 2.6 copy-start.14
  108.6 30.9 %copy-start.5 = (bf16[192,1792,1]{1,0,2:T(8,128)(2,1)}, bf16[192,1792,1]{1,0,2:T(8,128)(2,1)S(1)}, u32[]{:S(2)}) copy-start(bf16[192,1792,1]{1,0,2:T(8,128)(2,1)S(1)} %get-tuple-element.8) | copy-start | bytes 2064388
  108.6 30.0 %copy-start.22 = (f32[1,128]{1,0:T(1,128)S(1)}, f32[1,128]{1,0:T(1,128)}, u32[]{:S(2)}) copy-start(f32[1,128]{1,0:T(1,128)} %param.15) | copy-start | bytes 1540
  109.5 29.1 %copy-start.18 = (f32[192]{0:T(256)}, f32[192]{0:T(256)S(1)}, u32[]{:S(2)}) copy-start(f32[192]{0:T(256)S(1)} %add_rsqrt_fusion) | copy-start | bytes 2308
  138.4 18.0 %copy-start.7 = (bf16[1,3072,1,128]{3,1,2,0:T(8,128)(2,1)}, bf16[1,3072,1,128]{3,1,2,0:T(8,128)(2,1)S(1)}, u32[]{:S(2)}) copy-start(bf16[1,3072,1,128]{3,1,2,0:T(8,128)(2,1)S(1)} %all_gather.18) | copy-start | bytes 2359300
  138.6 22.6 %copy-start.19 = (f32[192]{0:T(256)}, f32[192]{0:T(256)S(1)}, u32[]{:S(2)}) copy-start(f32[192]{0:T(256)S(1)} %add_rsqrt_fusion.1) | copy-start | bytes 2308
  139.5 17.9 %copy-start.4 = (bf16[1,192,1792]{2,1,0:T(8,128)(2,1)S(1)}, bf16[1,192,1792]{2,1,0:T(8,128)(2,1)}, u32[]{:S(2)}) copy-start(bf16[1,192,1792]{2,1,0:T(8,128)(2,1)} %copy.28) | copy-start | bytes 2064388
  160.0 5.2 copy-start.12
  165.2 139.4 %reduce-scatter.14.cloned.1.call-start = ((), (), s32[]{:S(2)}) async-start(), calls=%async_computation.7 | async-start | bytes 2064384
  171.7 3.1 copy-start.23
  174.6 267.3 %all-gather.4.cloned.1.call-start = ((), (), s32[]{:S(2)}) async-start(), calls=%async_computation.6 | async-start | bytes 12386304 | tf_op jit(solution)/shard_map/all_gather | solution.py:158
  222.9 3.1 copy-start.13
  225.9 335.0 %reduce-scatter.16.cloned.1.call-start = ((), (), s32[]{:S(2)}) async-start(), calls=%async_computation.8 | async-start | bytes 946176
  228.5 458.1 %reduce-scatter.12.cloned.1.call-start = ((), (), s32[]{:S(2)}) async-start(), calls=%async_computation.5 | async-start | bytes 2838528 | tf_op jit(solution)/shard_map/reduce_scatter | solution.py:151
  441.9 6.0 copy-start.15
  447.9 3.9 copy-start.8
  447.9 3.9 copy-start.11
  (6 other events, 9.4 us)
Sparse Core Ops, SparseCore 0:
  165.3 55.2 reduce-scatter.9
  224.6 79.9 reduce-scatter.13
  307.2 134.6 all-gather.3
  444.8 116.0 reduce-scatter.15
  563.9 122.6 reduce-scatter.11
